TPU v7x, 32 devices: a whole 2x2x4 slice. The times are simulated.
32 devices in a mesh: dp: 16 (over z, x, core), fsdp: 2 (over y).
Axes of the slice: x: 2, y: 2, z: 4, core: 2. Of those that a mesh axis runs over, the one named last changes fastest.
Arguments:
- waveform: float32 [256, 400], P(('dp', 'fsdp')), may hold values from -6 to 6
- lengths: int32 [256], P(('dp', 'fsdp')), may hold values from 200 to 400, as said below
- owner_of: int32 [256], P(('dp', 'fsdp')), may hold values from 0 to 15, as said below
- targets: float32 [256, 39], P(('dp', 'fsdp')), may hold values from -5 to 5
- first_weight: float32 [10, 512], replicated, may hold values from -2 to 2
- first_gain: float32 [512], replicated, may hold values from 0.1 to 1.9
- first_shift: float32 [512], replicated, may hold values from -3 to 3
- second_weight: bfloat16 [1536, 512], P('fsdp'), may hold values from -0.15625 to 0.15625
- second_gain: float32 [512], replicated, may hold values from 0.1 to 1.9
- second_shift: float32 [512], replicated, may hold values from -3 to 3
Outputs:
- logvar: float32 [256, 39], P(('dp', 'fsdp'))
- loss: float32 [], replicated
- grad_second_weight: float32 [1536, 512], P('fsdp')
- grad_first_weight: float32 [10, 512], replicated
- grad_first_gain: float32 [512], replicated
- grad_first_shift: float32 [512], replicated
- grad_second_gain: float32 [512], replicated
- grad_second_shift: float32 [512], replicated
Inputs may be any that keep to these rules, and one draw needn't show every extreme that they name: `lengths`: every draw has a row of length 400 and one of length 200. `owner_of`: rows read by the devices of one fsdp index go to owners of the same fsdp index. From one reader, each owner receives either no row or exactly 1 row; every owner receives exactly 8 rows.
All inputs are finite; a program needn't handle non-finite values.
Results may differ from a plain program's by a relative error of at most 0.0019.
Values may be sent and summed in bfloat16 or wider, within the bound.
No kernel may reach another device: no remote copies, remote signals or barrier semaphores. Data moves between devices by JAX's collectives and lax.ppermute only.
A program may use at most 64 MiB of HBM per device.

v0:
```python
import jax
import jax.numpy as jnp
from jax import lax
from jax.sharding import PartitionSpec as P

epsilon = 1e-05


def layer_norm(values, norm_gain, norm_shift):
    row_mean = jnp.mean(values, axis=-1, keepdims=True)
    centered = values - row_mean
    row_var = jnp.mean(centered * centered, axis=-1, keepdims=True)
    return centered * lax.rsqrt(row_var + epsilon) * norm_gain + norm_shift


def first_layer(waveform, first_weight, first_gain, first_shift):
    row_total, samples = waveform.shape
    frames = samples // 5 - 1
    blocks = waveform.reshape(row_total, samples // 5, 5)
    windows = jnp.concatenate([blocks[:, :frames], blocks[:, 1 : frames + 1]], axis=2)
    pre_norm = jnp.dot(
        windows.reshape(row_total * frames, 10),
        first_weight,
        precision=lax.Precision.HIGHEST,
        preferred_element_type=jnp.float32,
    )
    return jax.nn.gelu(layer_norm(pre_norm, first_gain, first_shift), approximate=False)


def make_patches(activated, row_total):
    channels = activated.shape[1]
    frames = activated.shape[0] // row_total
    later = (frames - 1) // 2
    shaped = activated.reshape(row_total, frames, channels)
    padded = jnp.concatenate([shaped, jnp.zeros((row_total, 1, channels), activated.dtype)], axis=1)
    paired = padded.reshape(row_total, later + 1, 2, channels)
    even_frames = paired[:, :, 0]
    odd_frames = paired[:, :, 1]
    joined = jnp.concatenate(
        [even_frames[:, :later], odd_frames[:, :later], even_frames[:, 1:]], axis=2
    )
    return joined.reshape(row_total * later, 3 * channels)


def patch_grad(grad_patches, row_total, frames):
    channels = grad_patches.shape[1] // 3
    later = grad_patches.shape[0] // row_total
    shaped = grad_patches.reshape(row_total, later, 3, channels)
    zero_frame = jnp.zeros((row_total, 1, channels), grad_patches.dtype)
    even_frames = jnp.concatenate([shaped[:, :, 0], zero_frame], axis=1) + jnp.concatenate(
        [zero_frame, shaped[:, :, 2]], axis=1
    )
    odd_frames = jnp.concatenate([shaped[:, :, 1], zero_frame], axis=1)
    paired = jnp.stack([even_frames, odd_frames], axis=2).reshape(
        row_total, 2 * later + 2, channels
    )
    return paired[:, :frames].reshape(row_total * frames, channels)


def frame_mask_of(row_lengths, later):
    first_valid = (row_lengths - 10) // 5 + 1
    second_valid = (first_valid - 3) // 2 + 1
    inside = jnp.arange(later, dtype=jnp.int32)[None, :] < second_valid[:, None]
    return inside.astype(jnp.float32).reshape(-1)


def head_loss(second_pre, second_gain, second_shift, target_flat, frame_mask):
    activated = jax.nn.gelu(layer_norm(second_pre, second_gain, second_shift), approximate=False)
    row_mean = jnp.mean(activated, axis=-1, keepdims=True)
    centered = activated - row_mean
    raw_logvar = jnp.log(jnp.mean(centered * centered, axis=-1) + epsilon)
    misfit = raw_logvar - target_flat
    return (jnp.sum(frame_mask * misfit * misfit), raw_logvar)


def per_device(
    waveform,
    lengths,
    owner_of,
    targets,
    first_weight,
    first_gain,
    first_shift,
    second_weight,
    second_gain,
    second_shift,
):
    peer_count = lax.axis_size("dp")
    row_total, samples = waveform.shape
    later = targets.shape[1]
    frames = samples // 5 - 1
    per_owner = max(1, 2 * row_total // peer_count)
    slot_count = peer_count * per_owner
    matches = (owner_of[:, None] == owner_of[None, :]).astype(jnp.int32)
    earlier = jnp.sum(jnp.tril(matches, -1), axis=1)
    slot_index = owner_of * per_owner + earlier
    placing = (slot_index[:, None] == jnp.arange(slot_count, dtype=jnp.int32)[None, :]).astype(
        jnp.float32
    )
    sent_wave = lax.dot_general(
        placing,
        waveform,
        (((0,), (0,)), ((), ())),
        precision=lax.Precision.HIGHEST,
        preferred_element_type=jnp.float32,
    )
    sent_length = jnp.dot(
        lengths.astype(jnp.float32),
        placing,
        precision=lax.Precision.HIGHEST,
        preferred_element_type=jnp.float32,
    )
    got_wave, got_length = (
        lax.all_to_all(
            sent_wave.reshape(peer_count, per_owner, samples),
            "dp",
            split_axis=0,
            concat_axis=0,
            tiled=True,
        ),
        lax.all_to_all(
            sent_length.reshape(peer_count, per_owner),
            "dp",
            split_axis=0,
            concat_axis=0,
            tiled=True,
        ),
    )
    got_wave = got_wave.reshape(slot_count, samples)
    got_length = got_length.reshape(slot_count)
    present = got_length > 0.5
    arrival = jnp.cumsum(present.astype(jnp.int32)) - 1
    picking = (
        present[None, :] & (arrival[None, :] == jnp.arange(row_total, dtype=jnp.int32)[:, None])
    ).astype(jnp.float32)
    owned_wave = jnp.dot(
        picking, got_wave, precision=lax.Precision.HIGHEST, preferred_element_type=jnp.float32
    )
    owned_length = jnp.dot(
        picking, got_length, precision=lax.Precision.HIGHEST, preferred_element_type=jnp.float32
    ).astype(jnp.int32)

    def first_part(weight_first, gain_first, shift_first):
        return first_layer(owned_wave, weight_first, gain_first, shift_first)

    activated, first_pull = jax.vjp(first_part, first_weight, first_gain, first_shift)
    rounded = activated.astype(jnp.bfloat16)
    patches = make_patches(rounded, row_total)
    columns = patches
    second_pre = jnp.dot(
        columns,
        lax.all_gather(second_weight, "fsdp", axis=0, tiled=True),
        preferred_element_type=jnp.float32,
    )
    frame_mask = frame_mask_of(owned_length, later)

    def head_part(pre_norm, gain_second, shift_second):
        return head_loss(pre_norm, gain_second, shift_second, targets.reshape(-1), frame_mask)

    loss_sum, head_pull, raw_logvar = jax.vjp(
        head_part, second_pre, second_gain, second_shift, has_aux=True
    )
    grad_pre, grad_gain_two, grad_shift_two = head_pull(jnp.ones_like(loss_sum))
    grad_pre = grad_pre.astype(jnp.bfloat16)
    columns = patches
    grad_shard = lax.psum_scatter(
        lax.dot_general(
            columns, grad_pre, (((0,), (0,)), ((), ())), preferred_element_type=jnp.float32
        ).astype(jnp.bfloat16),
        "fsdp",
        scatter_dimension=0,
        tiled=True,
    ).astype(jnp.float32)
    grad_weight_two = lax.psum(grad_shard, "dp")
    grad_patches = lax.dot_general(
        grad_pre,
        lax.all_gather(second_weight, "fsdp", axis=0, tiled=True),
        (((1,), (1,)), ((), ())),
        preferred_element_type=jnp.float32,
    )
    grad_act = patch_grad(grad_patches, row_total, frames)
    grad_weight_one, grad_gain_one, grad_shift_one = first_pull(grad_act)
    summed = lax.psum(
        (
            grad_weight_one,
            grad_gain_one,
            grad_shift_one,
            grad_gain_two,
            grad_shift_two,
            loss_sum,
            jnp.sum(frame_mask),
        ),
        ("dp", "fsdp"),
    )
    logvar = (raw_logvar * frame_mask).reshape(row_total, later)
    loss = summed[5] / summed[6]
    return (logvar, loss, grad_weight_two, summed[0], summed[1], summed[2], summed[3], summed[4])


def solution(mesh):
    placed = (
        P(("dp", "fsdp"), None),
        P(("dp", "fsdp")),
        P(("dp", "fsdp")),
        P(("dp", "fsdp"), None),
        P(),
        P(),
        P(),
        P("fsdp", None),
        P(),
        P(),
    )
    return jax.shard_map(
        per_device,
        mesh=mesh,
        in_specs=placed,
        out_specs=(P(("dp", "fsdp"), None), P(), P("fsdp", None), P(), P(), P(), P(), P()),
        check_vma=False,
    )
```

profile of v0, /device:TPU:0, one launch (start us, length us, event | category | flops | bytes accessed | tf_op | source)
XLA Modules:
  0.0 200.0 jit_solution(7417395136879654368)
XLA Ops:
  7.2 0.9 select_reduce_fusion
  8.1 0.7 add.108
  8.8 1.5 fusion.21
  10.3 7.4 %all-to-all-start = ((f32[16,1,1]{2,1,0:T(1,128)}), f32[16,1,1]{2,1,0:T(1,128)S(1)}, u32[]{:S(2)}, u32[]{:S(2)}) async-start(f32[16,1,1]{2,1,0:T(1,128)} %bitcast.21), calls=%async_computation | async-start | bytes 16384 | tf_op jit(solution)/shard_map/all_to_all | solution.py:121
  17.7 0.7 all-gather.2.cloned.1.call-update
  18.4 1.0 convolution_bitcast_fusion
  19.4 0.7 copy.79
  20.0 0.8 reshape.196
  20.8 3.2 %all-to-all-done = f32[16,1,1]{2,1,0:T(1,128)S(1)} async-done(((f32[16,1,1]{2,1,0:T(1,128)}), f32[16,1,1]{2,1,0:T(1,128)S(1)}, u32[]{:S(2)}, u32[]{:S(2)}) %all-to-all-start) | async-done | bytes 96 | tf_op jit(solution)/shard_map/all_to_all | solution.py:121
  24.0 3.5 %all-to-all-start.1 = ((f32[16,1,400]{2,1,0:T(1,128)}), f32[16,1,400]{2,1,0:T(1,128)S(1)}, u32[]{:S(2)}, u32[]{:S(2)}) async-start(f32[16,1,400]{2,1,0:T(1,128)} %copy.79), calls=%async_computation.1 | async-start | bytes 65536 | tf_op jit(solution)/shard_map/all_to_all | solution.py:114
  27.6 0.2 reduce.2
  27.9 0.1 add_reduce_fusion
  28.0 0.1 fusion.38
  28.3 5.8 %all-to-all-done.1 = f32[16,1,400]{2,1,0:T(1,128)S(1)} async-done(((f32[16,1,400]{2,1,0:T(1,128)}), f32[16,1,400]{2,1,0:T(1,128)S(1)}, u32[]{:S(2)}, u32[]{:S(2)}) %all-to-all-start.1) | async-done | bytes 25632 | tf_op jit(solution)/shard_map/all_to_all | solution.py:114
  34.1 0.1 copy.92
  34.3 0.3 fusion.18
  34.9 1.3 fusion.55
  36.2 0.3 multiply_reduce_fusion.2
  36.5 4.4 %multiply_convert_fusion = (bf16[632,512]{1,0:T(8,128)(2,1)S(1)}, f32[632,512]{1,0:T(8,128)}) fusion(f32[632,512]{1,0:T(8,128)S(1)} %get-tuple-element.47, f32[512]{0:T(512)S(1)} %copy-done.6, f32[512]{0:T(512)S(1)} %copy-done.2, f32[632]{0:T(1024)S(1)} %fusion.26, f32[632]{0:T(1024)S(1)} %broadcast_multiply_fusion), kind=kLoop, calls=%fused_computation.10 | loop fusion | flops 22327296 | bytes 3244992 | tf_op jit(solution)/shard_map/convert_element_type | solution.py:147
  40.9 0.2 reshape.193
  41.2 0.2 reshape.194
  41.4 1.2 fusion.52
  42.6 0.2 copy_bitcast_fusion.3
  42.9 0.3 reshape.195
  43.3 5.4 %all-gather.2.cloned.1.call-done = bf16[1536,512]{1,0:T(8,128)(2,1)} async-done(((bf16[768,512]{1,0:T(8,128)(2,1)}), bf16[1536,512]{1,0:T(8,128)(2,1)}) %all-gather.2.cloned.1.call-update) | async-done | bytes 1572880 | tf_op jit(solution)/shard_map/all_gather | solution.py:152
  48.6 2.2 %fusion.56 = (f32[312]{0:T(512)S(1)}, f32[312,512]{1,0:T(8,128)S(1)}) fusion(bf16[312,1536]{1,0:T(8,128)(2,1)S(1)} %reshape.195, bf16[1536,512]{1,0:T(8,128)(2,1)} %all-gather.2.cloned.1.call-done), kind=kOutput, calls=%fused_computation.124 | convolution fusion | flops 490892992 | bytes 3171552 | tf_op jit(solution)/shard_map/dot_general | solution.py:150
  50.8 0.2 multiply_reduce_fusion.6
  51.1 1.7 fusion.48
  52.8 0.2 multiply_reduce_fusion.5
  53.0 0.3 fusion.17
  53.3 0.8 multiply_reduce_fusion.3
  54.1 0.3 fusion.47
  54.4 0.8 copy-done.1
  55.3 2.2 %convolution_convert_fusion = bf16[1536,512]{1,0:T(8,128)(2,1)} fusion(bf16[312,1536]{1,0:T(8,128)(2,1)S(1)} %reshape.195, f32[312,512]{1,0:T(8,128)S(1)} %get-tuple-element.27, f32[312]{0:T(512)S(1)} %negate_multiply_fusion.3), kind=kOutput, calls=%fused_computation | convolution fusion | flops 491839488 | bytes 3171552 | tf_op jit(solution)/shard_map/dot_general | solution.py:167
  57.5 2.3 %fusion.45 = f32[312,1536]{1,0:T(8,128)S(1)} fusion(bf16[1536,512]{1,0:T(8,128)(2,1)} %all-gather.2.cloned.1.call-done, f32[312,512]{1,0:T(8,128)} %copy-done.1, f32[312]{0:T(512)S(1)} %negate_multiply_fusion.3), kind=kOutput, calls=%fused_computation.115 | convolution fusion | flops 491053056 | bytes 4130016 | tf_op jit(solution)/shard_map/dot_general | solution.py:175
  59.8 2.7 %reshape.197 = f32[8,39,3,512]{3,2,1,0:T(4,128)} reshape(f32[312,1536]{1,0:T(8,128)S(1)} %fusion.45) | data formatting | bytes 3833856 | tf_op jit(solution)/shard_map/reshape | solution.py:48
  62.6 5.6 %fusion.51 = (f32[8,39,1,512]{3,2,1,0:T(1,128)S(1)}, f32[8,39,1,512]{3,2,1,0:T(1,128)S(1)}, f32[8,39,1,512]{3,2,1,0:T(1,128)S(1)}) fusion(f32[8,39,3,512]{3,2,1,0:T(4,128)} %reshape.197), kind=kLoop, calls=%fused_computation.119 | loop fusion | bytes 3833856 | tf_op jit(solution)/shard_map/slice | solution.py:50
  68.4 0.1 add_bitcast_fusion
  68.6 0.1 copy.87
  68.8 0.8 copy.88
  69.6 1.2 reshape.199
  70.9 2.9 %multiply_reduce_fusion = (f32[512]{0:T(512)S(1)}, f32[632]{0:T(1024)S(1)}, f32[512]{0:T(512)S(1)}, f32[632,512]{1,0:T(8,128)S(1)}) fusion(f32[632,512]{1,0:T(8,128)S(1)} %get-tuple-element.47, f32[632]{0:T(1024)S(1)} %fusion.26, f32[632]{0:T(1024)S(1)} %broadcast_multiply_fusion, f32[512]{0:T(512)S(1)} %copy-done.2, f32[632,512]{1,0:T(8,128)} %reshape.199, ...), kind=kLoop, calls=%fused_computation.5 | loop fusion | flops 7440776 | bytes 5193120 | tf_op jit(solution)/shard_map/transpose(jvp())/reduce_sum | solution.py:13
  73.8 0.5 fusion.46
  74.3 0.1 copy-done.4
  74.5 1.3 convert_reduce_fusion
  75.8 0.8 fusion.1
  76.7 40.4 %all-reduce.4 = (f32[]{:T(128)}, f32[]{:T(128)}, f32[10,512]{1,0:T(8,128)}, f32[512]{0:T(512)}, f32[512]{0:T(512)}, /*index=5*/f32[512]{0:T(512)}, f32[512]{0:T(512)}) all-reduce(f32[]{:T(128)} %get-tuple-element.15, f32[]{:T(128)} %get-tuple-element.14, f32[10,512]{1,0:T(8,128)S(1)} %fusion.1, ...), channel_id=1, replica_groups=mesh['dp'=16,'fsdp'=2] {'dp','fsdp'}, use_global_device_ids=true, to_apply=%region_9.10 | all-reduce | flops 7170 | bytes 57360 | tf_op jit(solution)/shard_map/psum | solution.py:183
  118.4 73.7 %all-reduce.6 = f32[768,512]{1,0:T(8,128)} all-reduce(bf16[768,512]{1,0:T(8,128)(2,1)} %reduce-scatter.2.cloned.1.call-done), channel_id=1, replica_groups=mesh['dp'=16,'fsdp'=2] {'dp'}, use_global_device_ids=true, to_apply=%region_16.17 | all-reduce | flops 393216 | bytes 2359296 | tf_op jit(solution)/shard_map/psum | solution.py:174
  (47 shorter events, 1.3 us)
Async XLA Ops:
  7.2 27.7 %copy-start = (f32[10,512]{1,0:T(8,128)S(1)}, f32[10,512]{1,0:T(8,128)}, u32[]{:S(2)}) copy-start(f32[10,512]{1,0:T(8,128)} %param.14) | copy-start | bytes 61444
  10.3 13.8 %all-to-all-start = ((f32[16,1,1]{2,1,0:T(1,128)}), f32[16,1,1]{2,1,0:T(1,128)S(1)}, u32[]{:S(2)}, u32[]{:S(2)}) async-start(f32[16,1,1]{2,1,0:T(1,128)} %bitcast.21), calls=%async_computation | async-start | bytes 16384 | tf_op jit(solution)/shard_map/all_to_all | solution.py:121
  17.7 31.0 %all-gather.2.cloned.1.call-start = ((), (), s32[]{:S(2)}) async-start(), calls=%async_computation.3 | async-start | bytes 2359296 | tf_op jit(solution)/shard_map/all_gather | solution.py:152
  24.0 10.1 %all-to-all-start.1 = ((f32[16,1,400]{2,1,0:T(1,128)}), f32[16,1,400]{2,1,0:T(1,128)S(1)}, u32[]{:S(2)}, u32[]{:S(2)}) async-start(f32[16,1,400]{2,1,0:T(1,128)} %copy.79), calls=%async_computation.1 | async-start | bytes 65536 | tf_op jit(solution)/shard_map/all_to_all | solution.py:114
  27.5 90.8 %reduce-scatter.2.cloned.1.call-start = ((), (), s32[]{:S(2)}) async-start(), calls=%async_computation.4 | async-start | bytes 2359296 | tf_op jit(solution)/shard_map/reduce_scatter | solution.py:166
  34.8 1.6 copy-start.2
  34.8 1.6 copy-start.6
  43.3 7.8 %copy-start.3 = (f32[512]{0:T(512)S(1)}, f32[512]{0:T(512)}, u32[]{:S(2)}) copy-start(f32[512]{0:T(512)} %param.18) | copy-start | bytes 6148
  43.3 7.8 %copy-start.5 = (f32[512]{0:T(512)S(1)}, f32[512]{0:T(512)}, u32[]{:S(2)}) copy-start(f32[512]{0:T(512)} %param.19) | copy-start | bytes 6148
  54.4 0.9 copy-start.1
  73.8 0.7 copy-start.4
Sparse Core Ops, SparseCore 0:
  20.0 28.5 all-gather.1
  57.6 26.1 reduce-scatter.1
where the time goes:
time: 201 us; the launch traced here: 200 us
  blocking collectives  114 us (57%)
  between operations  16.8 us (8%)
  local copies, waits for them, and re-layouts  15.8 us (8%)
  other arithmetic  15.4 us (8%)
  waiting for transfers between devices  15.2 us (8%)
  matrix products  11.8 us (6%)
  starting transfers between devices  11 us (5%)
    psum x1, blocking collectives, per_device(): grad_weight_two = lax.psum(grad_shard, 'dp')  73.7 us
    psum x1, blocking collectives, per_device(): lax.psum((grad_weight_one, grad_gain_one, grad_shift_one, grad_gain_two,...  40.4 us
    all_to_all x1, starting transfers between devices, per_device(): lax.all_to_all(sent_length.reshape(peer_count, per_owner), 'dp', split_ax...  7.39 us
    all_to_all x1, waiting for transfers between devices, per_device(): lax.all_to_all(sent_wave.reshape(peer_count, per_owner, samples), 'dp', s...  5.85 us
    slice x2, local copies, waits for them, and re-layouts, patch_grad(): shaped[:, :, 0]  5.62 us
    all_gather x1, waiting for transfers between devices, per_device(): lax.all_gather(second_weight, 'fsdp', axis=0, tiled=True)  5.37 us
    convert_element_type x1, other arithmetic, per_device(): rounded = activated.astype(jnp.bfloat16)  4.39 us
  transfers between devices with their start and end apart: 4, of which 3 were waited for; matrix products, arithmetic and copies ran while one was open for 15% of the time, Pallas kernels for 0%

commit v1 on v0

--- a/solution.py
+++ b/solution.py
@@ -1,9 +1,19 @@
+import functools
 import jax
 import jax.numpy as jnp
 from jax import lax
 from jax.sharding import PartitionSpec as P
+from jax.lax import all_gather
 
 epsilon = 1e-05
+
+
+def track_trees(row_data, net_axis):
+    last = all_gather(row_data, axis_name=net_axis).sum(axis=0)
+    return last
+
+
+_report_modes = functools.partial(track_trees, net_axis="dp")
 
 
 def layer_norm(values, norm_gain, norm_shift):
@@ -171,7 +181,7 @@
         scatter_dimension=0,
         tiled=True,
     ).astype(jnp.float32)
-    grad_weight_two = lax.psum(grad_shard, "dp")
+    grad_weight_two = _report_modes(grad_shard)
     grad_patches = lax.dot_general(
         grad_pre,
         lax.all_gather(second_weight, "fsdp", axis=0, tiled=True),

time: 201 us -> 228 us (1.13)
  waiting for transfers between devices: 15.2 us -> 99.9 us
  blocking collectives: 114 us -> 42.9 us
  other arithmetic: 15.4 us -> 28.8 us
    psum x1 -> x0, blocking collectives: 73.7 us -> none  [per_device(): grad_weight_two = lax.psum(grad_shard, 'dp')]
    all_gather x0 -> x1, waiting for transfers between devices: none -> 66 us  [track_trees(): last = all_gather(row_data, axis_name=net_axis).sum(axis=0)]
    reduce_scatter x1, waiting for transfers between devices: 0.02 us -> 23.4 us  [per_device(): lax.psum_scatter(lax.dot_general(columns, grad_pre, (((0,), (0,)), ((), (...]
    reduce_sum x0 -> x1, other arithmetic: none -> 10.9 us  [track_trees(): last = all_gather(row_data, axis_name=net_axis).sum(axis=0)]
    all_gather x1, waiting for transfers between devices: 5.37 us -> 0.02 us  [per_device(): lax.all_gather(second_weight, 'fsdp', axis=0, tiled=True)]
    all_gather x0 -> x1, other arithmetic: none -> 2.49 us  [track_trees(): last = all_gather(row_data, axis_name=net_axis).sum(axis=0)]
    psum x1, blocking collectives: 40.4 us -> 42.9 us  [per_device(): lax.psum((grad_weight_one, grad_gain_one, grad_shift_one, grad_gain_two,...]
  transfers between devices with their start and end apart: 4 -> 5, of which waited for: 3 -> 4; matrix products, arithmetic and copies ran while one was open for 15% -> 15% of each run, Pallas kernels for 0% -> 0%
where the time goes in v1:
time: 228 us; the launch traced here: 227 us
  waiting for transfers between devices  99.9 us (44%)
  blocking collectives  42.9 us (19%)
  other arithmetic  28.8 us (13%)
  between operations  16.5 us (7%)
  local copies, waits for them, and re-layouts  16.3 us (7%)
  matrix products  11.8 us (5%)
  starting transfers between devices  11.2 us (5%)
    all_gather x1, waiting for transfers between devices, track_trees(): last = all_gather(row_data, axis_name=net_axis).sum(axis=0)  66 us
    psum x1, blocking collectives, per_device(): lax.psum((grad_weight_one, grad_gain_one, grad_shift_one, grad_gain_two,...  42.9 us
    reduce_scatter x1, waiting for transfers between devices, per_device(): lax.psum_scatter(lax.dot_general(columns, grad_pre, (((0,), (0,)), ((), (...  23.4 us
    reduce_sum x1, other arithmetic, track_trees(): last = all_gather(row_data, axis_name=net_axis).sum(axis=0)  10.9 us
    all_to_all x1, starting transfers between devices, per_device(): lax.all_to_all(sent_length.reshape(peer_count, per_owner), 'dp', split_ax...  7.39 us
    slice x2, local copies, waits for them, and re-layouts, patch_grad(): shaped[:, :, 0]  6.15 us
    all_to_all x1, waiting for transfers between devices, per_device(): lax.all_to_all(sent_wave.reshape(peer_count, per_owner, samples), 'dp', s...  5.85 us
  transfers between devices with their start and end apart: 5, of which 4 were waited for; matrix products, arithmetic and copies ran while one was open for 15% of the time, Pallas kernels for 0%

profile of v1, /device:TPU:0, one launch (start us, length us, event | category | flops | bytes accessed | tf_op | source)
XLA Modules:
  0.0 227.4 jit_solution(13642651888016086005)
XLA Ops:
  7.2 0.7 all-gather.4.cloned.1.call-update
  7.9 0.9 select_reduce_fusion
  8.8 0.7 add.106
  9.5 1.5 fusion.21
  11.0 7.4 %all-to-all-start = ((f32[16,1,1]{2,1,0:T(1,128)}), f32[16,1,1]{2,1,0:T(1,128)S(1)}, u32[]{:S(2)}, u32[]{:S(2)}) async-start(f32[16,1,1]{2,1,0:T(1,128)} %bitcast.22), calls=%async_computation | async-start | bytes 16384 | tf_op jit(solution)/shard_map/all_to_all | solution.py:131
  18.4 1.0 convolution_bitcast_fusion
  19.4 0.8 reshape.196
  20.2 0.7 copy.79
  20.8 3.9 %all-to-all-done = f32[16,1,1]{2,1,0:T(1,128)S(1)} async-done(((f32[16,1,1]{2,1,0:T(1,128)}), f32[16,1,1]{2,1,0:T(1,128)S(1)}, u32[]{:S(2)}, u32[]{:S(2)}) %all-to-all-start) | async-done | bytes 96 | tf_op jit(solution)/shard_map/all_to_all | solution.py:131
  24.8 3.5 %all-to-all-start.1 = ((f32[16,1,400]{2,1,0:T(1,128)}), f32[16,1,400]{2,1,0:T(1,128)S(1)}, u32[]{:S(2)}, u32[]{:S(2)}) async-start(f32[16,1,400]{2,1,0:T(1,128)} %copy.79), calls=%async_computation.1 | async-start | bytes 65536 | tf_op jit(solution)/shard_map/all_to_all | solution.py:124
  28.5 0.2 reduce.2
  28.7 0.2 fusion.38
  29.0 5.8 %all-to-all-done.1 = f32[16,1,400]{2,1,0:T(1,128)S(1)} async-done(((f32[16,1,400]{2,1,0:T(1,128)}), f32[16,1,400]{2,1,0:T(1,128)S(1)}, u32[]{:S(2)}, u32[]{:S(2)}) %all-to-all-start.1) | async-done | bytes 25632 | tf_op jit(solution)/shard_map/all_to_all | solution.py:124
  34.9 0.1 copy.92
  35.0 0.3 fusion.18
  35.6 1.3 fusion.55
  36.9 0.3 multiply_reduce_fusion.2
  37.2 4.4 %multiply_convert_fusion = (bf16[632,512]{1,0:T(8,128)(2,1)S(1)}, f32[632,512]{1,0:T(8,128)}) fusion(f32[632,512]{1,0:T(8,128)S(1)} %get-tuple-element.47, f32[512]{0:T(512)S(1)} %copy-done.6, f32[512]{0:T(512)S(1)} %copy-done.2, f32[632]{0:T(1024)S(1)} %fusion.26, f32[632]{0:T(1024)S(1)} %broadcast_multiply_fusion), kind=kLoop, calls=%fused_computation.10 | loop fusion | flops 22327296 | bytes 3244992 | tf_op jit(solution)/shard_map/convert_element_type | solution.py:157
  41.7 0.2 reshape.193
  41.9 0.2 reshape.194
  42.2 1.2 fusion.52
  43.4 0.2 copy_bitcast_fusion.3
  43.7 0.3 reshape.195
  44.1 2.2 fusion.56
  46.3 0.2 multiply_reduce_fusion.6
  46.5 1.7 fusion.48
  48.2 0.2 multiply_reduce_fusion.5
  48.5 0.3 fusion.17
  48.8 0.8 multiply_reduce_fusion.3
  49.5 0.3 fusion.47
  49.9 0.8 copy-done.1
  50.7 2.2 convolution_convert_fusion
  52.9 0.2 all-gather.6.cloned.1.call-start
  53.2 23.4 %reduce-scatter.2.cloned.1.call-done = bf16[768,512]{1,0:T(8,128)(2,1)} async-done(((bf16[1536,512]{1,0:T(8,128)(2,1)}), bf16[768,512]{1,0:T(8,128)(2,1)}) %reduce-scatter.2.cloned.1.call-update) | async-done | bytes 786448 | tf_op jit(solution)/shard_map/reduce_scatter | solution.py:176
  76.5 2.5 %all_gather.17 = f32[768,512]{1,0:T(8,128)} convert(bf16[768,512]{1,0:T(8,128)(2,1)} %reduce-scatter.2.cloned.1.call-done) | non-fusion elementwise | flops 393216 | bytes 2359296 | tf_op jit(solution)/shard_map/all_gather | solution.py:12
  79.1 2.3 %fusion.45 = f32[312,1536]{1,0:T(8,128)S(1)} fusion(bf16[1536,512]{1,0:T(8,128)(2,1)} %all-gather.4.cloned.1.call-done, f32[312,512]{1,0:T(8,128)} %copy-done.1, f32[312]{0:T(512)S(1)} %negate_multiply_fusion.3), kind=kOutput, calls=%fused_computation.115 | convolution fusion | flops 491053056 | bytes 4130016 | tf_op jit(solution)/shard_map/dot_general | solution.py:185
  81.4 2.7 %reshape.197 = f32[8,39,3,512]{3,2,1,0:T(4,128)} reshape(f32[312,1536]{1,0:T(8,128)S(1)} %fusion.45) | data formatting | bytes 3833856 | tf_op jit(solution)/shard_map/reshape | solution.py:58
  84.2 6.1 %fusion.51 = (f32[8,39,1,512]{3,2,1,0:T(1,128)S(1)}, f32[8,39,1,512]{3,2,1,0:T(1,128)S(1)}, f32[8,39,1,512]{3,2,1,0:T(1,128)S(1)}) fusion(f32[8,39,3,512]{3,2,1,0:T(4,128)} %reshape.197), kind=kLoop, calls=%fused_computation.119 | loop fusion | bytes 3833856 | tf_op jit(solution)/shard_map/slice | solution.py:60
  91.0 0.8 copy.88
  91.7 1.2 reshape.199
  93.0 2.9 %multiply_reduce_fusion = (f32[512]{0:T(512)S(1)}, f32[632]{0:T(1024)S(1)}, f32[512]{0:T(512)S(1)}, f32[632,512]{1,0:T(8,128)S(1)}) fusion(f32[632,512]{1,0:T(8,128)S(1)} %get-tuple-element.47, f32[632]{0:T(1024)S(1)} %fusion.26, f32[632]{0:T(1024)S(1)} %broadcast_multiply_fusion, f32[512]{0:T(512)S(1)} %copy-done.2, f32[632,512]{1,0:T(8,128)} %reshape.199, ...), kind=kLoop, calls=%fused_computation.5 | loop fusion | flops 7440776 | bytes 5193120 | tf_op jit(solution)/shard_map/transpose(jvp())/reduce_sum | solution.py:23
  95.9 0.5 fusion.46
  96.4 0.1 copy-done.4
  96.6 1.3 convert_reduce_fusion
  97.8 0.8 fusion.1
  98.7 42.9 %all-reduce.4 = (f32[]{:T(128)}, f32[]{:T(128)}, f32[10,512]{1,0:T(8,128)}, f32[512]{0:T(512)}, f32[512]{0:T(512)}, /*index=5*/f32[512]{0:T(512)}, f32[512]{0:T(512)}) all-reduce(f32[]{:T(128)} %get-tuple-element.15, f32[]{:T(128)} %get-tuple-element.14, f32[10,512]{1,0:T(8,128)S(1)} %fusion.1, ...), channel_id=1, replica_groups=mesh['dp'=16,'fsdp'=2] {'dp','fsdp'}, use_global_device_ids=true, to_apply=%region_9.10 | all-reduce | flops 7170 | bytes 57360 | tf_op jit(solution)/shard_map/psum | solution.py:193
  142.8 66.0 %all-gather.6.cloned.1.call-done = f32[12288,512]{1,0:T(8,128)} async-done(((f32[768,512]{1,0:T(8,128)}), f32[12288,512]{1,0:T(8,128)}) %all-gather.6.cloned.1.call-update) | async-done | bytes 25165840 | tf_op jit(solution)/shard_map/all_gather | solution.py:12
  208.8 10.9 %reduce_sum.188 = f32[768,512]{1,0:T(8,128)} reduce(f32[16,768,512]{2,1,0:T(8,128)} %bitcast.60, f32[]{:T(128)} %constant.48.clone.1), dimensions={0}, to_apply=%region_16.17 | reduce | flops 5898240 | bytes 26738692 | tf_op jit(solution)/shard_map/reduce_sum | solution.py:12
  (51 shorter events, 1.7 us)
Async XLA Ops:
  7.2 28.4 %copy-start = (f32[10,512]{1,0:T(8,128)S(1)}, f32[10,512]{1,0:T(8,128)}, u32[]{:S(2)}) copy-start(f32[10,512]{1,0:T(8,128)} %param.14) | copy-start | bytes 61444
  7.2 36.9 %all-gather.4.cloned.1.call-start = ((), (), s32[]{:S(2)}) async-start(), calls=%async_computation.3 | async-start | bytes 2359296 | tf_op jit(solution)/shard_map/all_gather | solution.py:162
  11.0 13.8 %all-to-all-start = ((f32[16,1,1]{2,1,0:T(1,128)}), f32[16,1,1]{2,1,0:T(1,128)S(1)}, u32[]{:S(2)}, u32[]{:S(2)}) async-start(f32[16,1,1]{2,1,0:T(1,128)} %bitcast.22), calls=%async_computation | async-start | bytes 16384 | tf_op jit(solution)/shard_map/all_to_all | solution.py:131
  24.8 10.1 %all-to-all-start.1 = ((f32[16,1,400]{2,1,0:T(1,128)}), f32[16,1,400]{2,1,0:T(1,128)S(1)}, u32[]{:S(2)}, u32[]{:S(2)}) async-start(f32[16,1,400]{2,1,0:T(1,128)} %copy.79), calls=%async_computation.1 | async-start | bytes 65536 | tf_op jit(solution)/shard_map/all_to_all | solution.py:124
  28.3 48.3 %reduce-scatter.2.cloned.1.call-start = ((), (), s32[]{:S(2)}) async-start(), calls=%async_computation.4 | async-start | bytes 2359296 | tf_op jit(solution)/shard_map/reduce_scatter | solution.py:176
  35.6 1.6 copy-start.2
  35.6 1.6 copy-start.6
  44.0 2.5 %copy-start.3 = (f32[512]{0:T(512)S(1)}, f32[512]{0:T(512)}, u32[]{:S(2)}) copy-start(f32[512]{0:T(512)} %param.18) | copy-start | bytes 6148
  44.0 2.5 %copy-start.5 = (f32[512]{0:T(512)S(1)}, f32[512]{0:T(512)}, u32[]{:S(2)}) copy-start(f32[512]{0:T(512)} %param.19) | copy-start | bytes 6148
  49.9 0.8 copy-start.1
  52.9 155.9 %all-gather.6.cloned.1.call-start = ((), (), s32[]{:S(2)}) async-start(), calls=%async_computation.5 | async-start | bytes 26738688 | tf_op jit(solution)/shard_map/all_gather | solution.py:12
  95.9 0.7 copy-start.4
Sparse Core Ops, SparseCore 0:
  9.5 29.9 all-gather.3
  53.1 23.4 reduce-scatter.1
  79.2 129.6 all-gather.5
